TPU v7x, 256 devices: a whole 4x4x8 slice. The times are simulated.
256 devices in a mesh: days: 4 (over y), space: 64 (over z, x, core).
Axes of the slice: x: 4, y: 4, z: 8, core: 2. Of those that a mesh axis runs over, the one named last changes fastest.
Arguments:
- fields: bfloat16 [640, 256, 1440], P('days', 'space')
- month_label: int32 [640], P('days'), may hold values from 0 to 11, as said below
- row_index: int32 [256], P('space'), may hold values from 0 to 255
- area_table: float32 [256], replicated, may hold values from 0.05 to 1
- basis: bfloat16 [64, 256, 1440], P(None, 'space'), may hold values from -6 to 6
Outputs:
- eofs: float32 [64, 256, 1440], P(None, 'space')
- pcs: float32 [640, 64], P('days')
Inputs may be any that keep to these rules, and one draw needn't show every extreme that they name: `month_label`: each day's label differs from floor(12 * day / 640) by at most one; the first day with a given value of floor(12 * day / 640) carries exactly that value; every month labels at least one day.
All inputs are finite; a program needn't handle non-finite values.
Results may differ from a plain program's by a relative error of at most 0.0003.
Values sent between devices are 32-bit elements; how exact they have to be, the bound alone decides.
No kernel may reach another device: no remote copies, remote signals or barrier semaphores. Data moves between devices by JAX's collectives and lax.ppermute only.
A program may use at most 64 MiB of HBM per device.

v0:
```python
import jax
import jax.numpy as jnp
from jax import lax
from jax.sharding import PartitionSpec as P

MONTHS = 12
LANES = 128
SIDE = 128
HIGH = lax.Precision.HIGHEST


def to_each(shard, axis):
    devices = lax.axis_size(axis)
    return lax.all_to_all(
        jnp.broadcast_to(shard[None], (devices, *shard.shape)), axis, 0, 0, tiled=True
    )


def summed(tiles, axis):
    return jnp.sum(lax.all_to_all(tiles, axis, 0, 0, tiled=True), axis=0)


def total_everywhere(rows):
    days, space = lax.axis_size("days"), lax.axis_size("space")
    count = rows.shape[0]
    rows = jnp.pad(rows, ((0, -count % (days * space)), (0, 0)))
    part = summed(rows.reshape(days, -1, LANES), "days")
    own = summed(part.reshape(space, 1, -1), "space")
    part = to_each(own, "space").reshape(-1, LANES)
    return to_each(part, "days").reshape(-1, LANES)[:count]


def dot(a, b, dims):
    return lax.dot_general(
        a, b, (dims, ((), ())), precision=HIGH, preferred_element_type=jnp.float32
    )


def pair_blocks(weighted):
    blocks = [weighted[at : at + SIDE] for at in range(0, weighted.shape[0], SIDE)]
    n = len(blocks)
    ahead = n // 2 + 1
    return n, [
        dot(blocks[i], blocks[(i + j) % n], ((1,), (1,))) for i in range(n) for j in range(ahead)
    ]


def whole_of(blocks, n):
    ahead = n // 2 + 1
    grid = [[None] * n for _ in range(n)]
    for i in range(n):
        for j in range(ahead):
            k = (i + j) % n
            block = blocks[i * ahead + j]
            grid[i][k] = block
            if j:
                grid[k][i] = block.T
    return jnp.concatenate([jnp.concatenate(line, axis=1) for line in grid], axis=0)


def inverse_of(lower):
    return lax.linalg.triangular_solve(
        lower, jnp.eye(lower.shape[0], dtype=lower.dtype), left_side=True, lower=True
    )


def local(fields, month_label, row_index, area_table, basis):
    days, lat, lon = fields.shape
    groups = lax.axis_size("days")
    me = lax.axis_index("days")
    wide = -(-(lon + 1) // LANES) * LANES
    modes = basis.shape[0]
    days_total = days * groups

    label = jnp.broadcast_to(month_label.astype(jnp.float32)[None, :, None], (lat, days, 1))
    rows = jnp.concatenate(
        [jnp.swapaxes(fields, 0, 1).astype(jnp.float32), label], axis=2
    )
    rows = jnp.pad(rows, ((0, 0), (0, 0), (0, wide - lon - 1)))
    rows = lax.all_to_all(rows, "days", 0, 0, tiled=True).reshape(days_total, wide)

    months = jnp.arange(MONTHS, dtype=jnp.float32)
    onehot = (rows[:, lon][None, :] == months[:, None]).astype(jnp.float32)
    own = jnp.where(jnp.arange(wide) < lon, rows, 0.0)
    sums = dot(onehot, own, ((1,), (0,)))
    climate = sums / jnp.sum(onehot, axis=1)[:, None]
    seasonal = dot(onehot, climate, ((0,), (0,)))
    table_row = lax.dynamic_index_in_dim(row_index, me, keepdims=False)
    area = jnp.sum(jnp.where(jnp.arange(area_table.shape[0]) == table_row, area_table, 0.0))
    weighted = (own - seasonal) * jnp.sqrt(area)

    start = lax.dynamic_index_in_dim(basis, me, axis=1, keepdims=False).astype(jnp.float32)
    start = jnp.pad(start, ((0, 0), (0, wide - lon)))
    start_pcs = dot(start, weighted, ((1,), (1,)))
    n, blocks = pair_blocks(weighted)
    pieces = blocks + [start_pcs[:, at : at + SIDE] for at in range(0, days_total, SIDE)]
    rows = total_everywhere(jnp.concatenate(pieces, axis=0))

    count = len(blocks)
    blocks = [rows[i * SIDE : (i + 1) * SIDE] for i in range(count)]
    rest = rows[count * SIDE :].reshape(n, modes, SIDE)
    pcs = jnp.moveaxis(rest, 0, 1).reshape(modes, days_total)
    products = whole_of(blocks, n) / days_total

    raw = dot(pcs, products, ((1,), (0,)))
    raw_cover = dot(raw, weighted, ((1,), (0,))) / days_total
    cover = to_each(raw_cover[:, :lon], "days")

    first = inverse_of(jnp.linalg.cholesky(dot(pcs, raw, ((1,), (1,))) / days_total))
    pcs = dot(first, raw, ((1,), (0,)))
    raw = dot(pcs, products, ((1,), (0,)))
    second = inverse_of(jnp.linalg.cholesky(dot(pcs, raw, ((1,), (1,))) / days_total))
    both = dot(second, first, ((1,), (0,)))
    eofs = jnp.einsum("kj,ljc->klc", both, cover, precision=HIGH)
    mine = lax.dynamic_slice_in_dim(raw, me * days, days, axis=1)
    return (eofs, dot(mine, second, ((0,), (1,))))


def solution(mesh):
    placed = (P("days", "space", None), P("days"), P("space"), P(), P(None, "space", None))
    return jax.shard_map(
        local,
        mesh=mesh,
        in_specs=placed,
        out_specs=(P(None, "space", None), P("days", None)),
        check_vma=False,
    )
```

profile of v0, /device:TPU:1, one launch (start us, length us, event | category | flops | bytes accessed | tf_op | source)
XLA Modules:
  0.0 222.6 jit_solution(2136188162420426967)
XLA Ops:
  0.7 2.2 convert_bitcast_fusion
  3.0 2.4 %select_maximum_fusion = f32[4,160,1536]{2,1,0:T(8,128)} fusion(f32[4,160,1]{2,1,0:T(8,128)S(1)} %broadcast_in_dim.23, f32[4,160,1440]{2,1,0:T(8,128)S(1)} %convert_bitcast_fusion), kind=kLoop, calls=%fused_computation | loop fusion | flops 3932160 | bytes 7621120 | tf_op jit(solution)/shard_map/concatenate | solution.py:76
  5.3 5.1 %all-to-all-start = ((f32[4,160,1536]{2,1,0:T(8,128)}), f32[4,160,1536]{2,1,0:T(8,128)}, u32[]{:S(2)}, u32[]{:S(2)}) async-start(f32[4,160,1536]{2,1,0:T(8,128)} %select_maximum_fusion), calls=%async_computation | async-start | bytes 7864320 | tf_op jit(solution)/shard_map/all_to_all | solution.py:80
  11.1 1.2 fusion.60
  13.5 41.3 %all-to-all-done = f32[4,160,1536]{2,1,0:T(8,128)} async-done(((f32[4,160,1536]{2,1,0:T(8,128)}), f32[4,160,1536]{2,1,0:T(8,128)}, u32[]{:S(2)}, u32[]{:S(2)}) %all-to-all-start) | async-done | bytes 3932192 | tf_op jit(solution)/shard_map/all_to_all | solution.py:80
  54.8 1.2 slice_reduce_fusion
  56.2 3.6 %fusion.2 = f32[12,1536]{1,0:T(8,128)S(1)} fusion(f32[640,1536]{1,0:T(8,128)} %bitcast.1, pred[1536]{0:T(1024)(128)(4,1)S(1)} %iota_compare_fusion.8, f32[12]{0:T(128)S(1)} %convert_reduce_fusion, f32[640]{0:T(1024)S(1)} %slice_reduce_fusion), kind=kOutput, calls=%fused_computation.6 | convolution fusion | flops 142566912 | bytes 4010032 | tf_op jit(solution)/shard_map/dot_general | solution.py:34
  59.8 4.1 %subtract_multiply_fusion = f32[640,1536]{1,0:T(8,128)S(1)} fusion(f32[640,1536]{1,0:T(8,128)} %bitcast.1, f32[12,1536]{1,0:T(8,128)S(1)} %fusion.2, f32[]{:T(128)S(6)} %sqrt.3, pred[1536]{0:T(1024)(128)(4,1)S(1)} %iota_compare_fusion.8, f32[640]{0:T(1024)S(1)} %slice_reduce_fusion), kind=kOutput, calls=%fused_computation.3 | convolution fusion | flops 144514560 | bytes 7942148 | tf_op jit(solution)/shard_map/dot_general | solution.py:34
  64.7 0.8 convolution_dynamic-update-slice_fusion.13
  65.5 0.8 convolution_dynamic-update-slice_fusion.12
  67.1 0.8 convolution_dynamic-update-slice_fusion.10
  67.9 0.8 convolution_dynamic-update-slice_fusion.9
  69.4 0.8 convolution_dynamic-update-slice_fusion.7
  70.2 0.8 convolution_dynamic-update-slice_fusion.6
  71.0 0.8 convolution_dynamic-update-slice_fusion.5
  71.8 0.8 convolution_dynamic-update-slice_fusion.4
  72.6 1.0 convolution_dynamic-update-slice_fusion.3
  74.4 0.8 convolution_dynamic-update-slice_fusion.1
  75.2 0.8 convolution_dynamic-update-slice_fusion
  76.0 2.1 fusion.38
  78.3 15.8 %all_to_all.30 = f32[4,576,128]{2,1,0:T(8,128)S(1)} all-to-all(f32[4,576,128]{2,1,0:T(8,128)S(1)} %bitcast.89), channel_id=1, replica_groups=mesh['days'=4,'space'=64] {'days'}, dimensions={0} | all-to-all | bytes 2359296 | tf_op jit(solution)/shard_map/all_to_all | solution.py:20
  94.1 30.9 %all_to_all.31 = f32[64,1,1152]{2,1,0:T(1,128)S(1)} all-to-all(f32[64,1,1152]{2,1,0:T(1,128)S(1)} %bitcast.92), channel_id=1, replica_groups=mesh['days'=4,'space'=64] {'space'}, dimensions={0} | all-to-all | bytes 589824 | tf_op jit(solution)/shard_map/all_to_all | solution.py:20
  125.4 18.3 %all_to_all.32 = f32[64,1,1152]{2,1,0:T(1,128)S(1)} all-to-all(f32[64,1,1152]{2,1,0:T(1,128)S(1)} %broadcast_in_dim.44), channel_id=1, replica_groups=mesh['days'=4,'space'=64] {'space'}, dimensions={0} | all-to-all | bytes 589824 | tf_op jit(solution)/shard_map/all_to_all | solution.py:14
  143.7 1.1 broadcast_in_dim.46
  144.8 3.7 %all-to-all-start.4 = ((f32[4,576,128]{2,1,0:T(8,128)}), f32[4,576,128]{2,1,0:T(8,128)S(1)}, u32[]{:S(2)}, u32[]{:S(2)}) async-start(f32[4,576,128]{2,1,0:T(8,128)} %broadcast_in_dim.46), calls=%async_computation.4 | async-start | bytes 2359296 | tf_op jit(solution)/shard_map/all_to_all | solution.py:14
  148.5 16.2 %all-to-all-done.4 = f32[4,576,128]{2,1,0:T(8,128)S(1)} async-done(((f32[4,576,128]{2,1,0:T(8,128)}), f32[4,576,128]{2,1,0:T(8,128)S(1)}, u32[]{:S(2)}, u32[]{:S(2)}) %all-to-all-start.4) | async-done | bytes 1179680 | tf_op jit(solution)/shard_map/all_to_all | solution.py:14
  166.1 0.8 slice_dynamic-update-slice_fusion.2
  166.9 0.8 slice_dynamic-update-slice_fusion.5
  167.8 0.8 slice_dynamic-update-slice_fusion.4
  168.8 0.9 slice_bitcast_fusion.1
  169.8 0.8 slice_dynamic-update-slice_fusion.1
  170.6 0.8 slice_dynamic-update-slice_fusion.3
  171.5 0.8 constant_dynamic-update-slice_fusion.15
  172.3 0.9 slice_bitcast_fusion
  173.3 0.8 slice_dynamic-update-slice_fusion
  174.2 1.1 fusion.9
  175.5 4.6 %fusion.68 = f32[64,1536]{1,0:T(8,128)S(1)} fusion(f32[64,640]{1,0:T(8,128)S(1)} %fusion.9, f32[640,1536]{1,0:T(8,128)} %copy-done.1), kind=kOutput, calls=%fused_computation.139 | convolution fusion | flops 754974720 | bytes 4489216 | tf_op jit(solution)/shard_map/dot_general | solution.py:34
  180.2 5.8 %cholesky.44 = f32[64,64]{1,0:T(8,128)S(1)} custom-call(f32[64,64]{1,0:T(8,128)S(1)} %fusion.55), custom_call_target="Cholesky" | custom-call | tf_op jit(solution)/shard_map/jit(cholesky)/cholesky | solution.py:109
  187.4 4.9 %custom-call.6 = f32[1,64,64]{1,2,0:T(8,128)S(1)} custom-call(f32[1,64,64]{2,1,0:T(8,128)S(1)} %fusion.50), custom_call_target="InvertDiagBlocksLowerTriangular" | custom-call | tf_op jit(solution)/shard_map/triangular_solve/custom-call.0 | solution.py:62
  192.9 1.1 fusion.7
  194.3 1.3 broadcast_in_dim.47
  195.7 3.8 %all-to-all-start.5 = ((f32[4,64,1440]{2,1,0:T(8,128)}), f32[4,64,1440]{2,1,0:T(8,128)S(1)}, u32[]{:S(2)}, u32[]{:S(2)}) async-start(f32[4,64,1440]{2,1,0:T(8,128)} %broadcast_in_dim.47), calls=%async_computation.5 | async-start | bytes 3145728 | tf_op jit(solution)/shard_map/all_to_all | solution.py:14
  199.5 5.8 %cholesky.55 = f32[64,64]{1,0:T(8,128)S(1)} custom-call(f32[64,64]{1,0:T(8,128)S(1)} %fusion.53), custom_call_target="Cholesky" | custom-call | tf_op jit(solution)/shard_map/jit(cholesky)/cholesky | solution.py:112
  206.7 4.9 %custom-call.7 = f32[1,64,64]{1,2,0:T(8,128)S(1)} custom-call(f32[1,64,64]{2,1,0:T(8,128)S(1)} %fusion.51), custom_call_target="InvertDiagBlocksLowerTriangular" | custom-call | tf_op jit(solution)/shard_map/triangular_solve/custom-call.0 | solution.py:62
  212.0 0.9 fusion.44
  212.9 6.0 %all-to-all-done.5 = f32[4,64,1440]{2,1,0:T(8,128)S(1)} async-done(((f32[4,64,1440]{2,1,0:T(8,128)}), f32[4,64,1440]{2,1,0:T(8,128)S(1)}, u32[]{:S(2)}, u32[]{:S(2)}) %all-to-all-start.5) | async-done | bytes 1474592 | tf_op jit(solution)/shard_map/all_to_all | solution.py:14
  219.0 1.5 fusion.69
  220.5 2.2 copy.108
  (78 shorter events, 10.9 us)
Async XLA Ops:
  0.6 12.4 %copy-start = (bf16[64,4,1440]{2,1,0:T(4,128)(2,1)S(1)}, bf16[64,4,1440]{2,1,0:T(4,128)(2,1)}, u32[]{:S(2)}) copy-start(bf16[64,4,1440]{2,1,0:T(4,128)(2,1)} %param.12) | copy-start | bytes 2211844
  0.6 2.2 copy-start.3
  5.3 5.1 %copy-start.5 = (s32[4]{0:T(128)S(1)}, s32[4]{0:T(128)}, u32[]{:S(2)}) copy-start(s32[4]{0:T(128)} %param.10) | copy-start | bytes 52
  5.3 5.7 %copy-start.4 = (f32[256]{0:T(256)S(1)}, f32[256]{0:T(256)}, u32[]{:S(2)}) copy-start(f32[256]{0:T(256)} %param.11) | copy-start | bytes 3076
  5.3 49.4 %all-to-all-start = ((f32[4,160,1536]{2,1,0:T(8,128)}), f32[4,160,1536]{2,1,0:T(8,128)}, u32[]{:S(2)}, u32[]{:S(2)}) async-start(f32[4,160,1536]{2,1,0:T(8,128)} %select_maximum_fusion), calls=%async_computation | async-start | bytes 7864320 | tf_op jit(solution)/shard_map/all_to_all | solution.py:80
  63.9 12.1 %copy-start.1 = (f32[640,1536]{1,0:T(8,128)}, f32[640,1536]{1,0:T(8,128)S(1)}, u32[]{:S(2)}) copy-start(f32[640,1536]{1,0:T(8,128)S(1)} %subtract_multiply_fusion) | copy-start | bytes 11796484
  144.8 19.9 %all-to-all-start.4 = ((f32[4,576,128]{2,1,0:T(8,128)}), f32[4,576,128]{2,1,0:T(8,128)S(1)}, u32[]{:S(2)}, u32[]{:S(2)}) async-start(f32[4,576,128]{2,1,0:T(8,128)} %broadcast_in_dim.46), calls=%async_computation.4 | async-start | bytes 2359296 | tf_op jit(solution)/shard_map/all_to_all | solution.py:14
  164.7 1.0 copy-start.2
  195.7 23.3 %all-to-all-start.5 = ((f32[4,64,1440]{2,1,0:T(8,128)}), f32[4,64,1440]{2,1,0:T(8,128)S(1)}, u32[]{:S(2)}, u32[]{:S(2)}) async-start(f32[4,64,1440]{2,1,0:T(8,128)} %broadcast_in_dim.47), calls=%async_computation.5 | async-start | bytes 3145728 | tf_op jit(solution)/shard_map/all_to_all | solution.py:14
where the time goes:
time: 224 us; the launch traced here: 223 us
  blocking collectives  65 us (29%)
  waiting for transfers between devices  63.5 us (28%)
  matrix products  32.5 us (15%)
  other arithmetic  30.4 us (14%)
  local copies, waits for them, and re-layouts  16.6 us (7%)
  starting transfers between devices  12.7 us (6%)
    all_to_all x2, blocking collectives, summed(): return jnp.sum(lax.all_to_all(tiles, axis, 0, 0, tiled=True), axis=0)  46.6 us
    all_to_all x1, waiting for transfers between devices, local(): lax.all_to_all(rows, 'days', 0, 0, tiled=True).reshape(days_total, wide)  41.3 us
    dot_general x26, matrix products, dot(): lax.dot_general(a, b, (dims, ((), ())), precision=HIGH, preferred_element...  30.5 us
    all_to_all x2, waiting for transfers between devices, to_each(): lax.all_to_all(jnp.broadcast_to(shard[None], (devices, *shard.shape)), ax...  22.2 us
    all_to_all x1, blocking collectives, to_each(): lax.all_to_all(jnp.broadcast_to(shard[None], (devices, *shard.shape)), ax...  18.3 us
    another operation x6, other arithmetic, local(): jnp.linalg.cholesky(dot(pcs, raw, ((1,), (1,))) / days_total)  13 us
    another operation x4, other arithmetic, inverse_of(): lax.linalg.triangular_solve(lower, jnp.eye(lower.shape[0], dtype=lower.dt...  11.1 us
    unnamed x46, local copies, waits for them, and re-layouts  8.32 us
  transfers between devices with their start and end apart: 3, of which 3 were waited for; matrix products, arithmetic and copies ran while one was open for 7% of the time, Pallas kernels for 0%

commit v1 on v0

v1 whole, which is shorter than its diff:
```python
import functools

import jax
import jax.numpy as jnp
from jax import lax
from jax.experimental import pallas as pl
from jax.experimental.pallas import tpu as pltpu
from jax.sharding import Mesh, PartitionSpec as P

MONTHS = 12
LANES = 128
SIDE = 128
HIGH = lax.Precision.HIGHEST
F32 = jnp.float32
BF16 = jnp.bfloat16
INTERPRET = False
SPACE = ("z", "x", "core")
STAGES = ("core", ("days", "x"), "z")


def to_each(shard, axis):
    devices = lax.axis_size(axis)
    return lax.all_to_all(
        jnp.broadcast_to(shard[None], (devices, *shard.shape)), axis, 0, 0, tiled=True
    )


def total_everywhere(rows):
    for axis in STAGES:
        devices = lax.axis_size(axis)
        share = rows.shape[0] // devices
        shape = (devices, 1, share * LANES) if share % 8 else (devices, share, LANES)
        tiles = lax.all_to_all(rows.reshape(shape), axis, 0, 0, tiled=True)
        rows = jnp.sum(tiles, axis=0).reshape(share, LANES)
    for axis in STAGES[::-1]:
        flat = rows.reshape(1, -1) if rows.shape[0] % 8 else rows
        rows = to_each(flat, axis).reshape(-1, LANES)
    return rows


def dot(a, b, dims, precision=HIGH):
    return lax.dot_general(a, b, (dims, ((), ())), precision=precision, preferred_element_type=F32)


def one_pass(a, b, dims):
    return dot(a, b, dims, lax.Precision.DEFAULT)


NT = ((1,), (1,))
NN = ((1,), (0,))


def split(x):
    high = x.astype(BF16)
    return high, (x - high.astype(F32)).astype(BF16)


def runs(first, count, n):
    head = min(count, n - first)
    found = [(first, 0, head)]
    if head < count:
        found.append((0, head, count - head))
    return found


def products_kernel(lon, rows_ref, base_ref, scale_ref, out_ref, high_ref, low_ref):
    days, wide = rows_ref.shape
    modes = base_ref.shape[0]
    n = days // SIDE
    ahead = n // 2 + 1
    at_label = lon // LANES * LANES
    label = rows_ref[:, at_label : at_label + LANES][:, lon - at_label : lon - at_label + 1]
    lane = lax.broadcasted_iota(jnp.int32, (days, LANES), 1)
    thrice = ((lane % 16).astype(F32) == label) & (lane < 48)
    thrice = jnp.where(thrice, 1.0, 0.0)
    hot = jnp.transpose(thrice)[:16]
    counts = jnp.sum(hot, axis=1, keepdims=True)
    sums = one_pass(hot.astype(BF16), rows_ref[...].astype(BF16), NN)
    climate = sums / jnp.maximum(counts, 1.0)
    first, rest = split(climate)
    rest = climate - first.astype(F32)
    second = rest.astype(BF16)
    third = (rest - second.astype(F32)).astype(BF16)
    terms = jnp.concatenate(
        [first.astype(F32), second.astype(F32), third.astype(F32), jnp.zeros((LANES - 48, wide), F32)]
    ).astype(BF16)
    inside = lax.broadcasted_iota(jnp.int32, (SIDE, wide), 1) < lon
    scale = scale_ref[0, 0]
    for i in range(n):
        part = slice(i * SIDE, (i + 1) * SIDE)
        seasonal = one_pass(thrice[part].astype(BF16), terms, NN)
        weighted = jnp.where(inside, (rows_ref[part] - seasonal) * scale, 0.0)
        high, low = split(weighted)
        high_ref[part] = high
        low_ref[part] = low
    for i in range(n):
        part = slice(i * SIDE, (i + 1) * SIDE)
        for block, offset, length in runs(i, ahead, n):
            other = slice(block * SIDE, (block + length) * SIDE)
            product = one_pass(high_ref[part], high_ref[other], NT)
            product += one_pass(high_ref[part], low_ref[other], NT)
            product += one_pass(low_ref[part], high_ref[other], NT)
            for j in range(length):
                at = (i * ahead + offset + j) * SIDE
                out_ref[at : at + SIDE] = product[:, j * SIDE : (j + 1) * SIDE]
    pcs = one_pass(base_ref[...], high_ref[...], NT) + one_pass(base_ref[...], low_ref[...], NT)
    at = n * ahead * SIDE
    for i in range(n):
        out_ref[at : at + modes] = pcs[:, i * SIDE : (i + 1) * SIDE]
        at += modes
    if at < out_ref.shape[0]:
        out_ref[at:] = jnp.zeros((out_ref.shape[0] - at, LANES), F32)


def cover_kernel(rows_ref, high_ref, low_ref, products_ref, pcs_ref, raw_ref, cover_ref):
    modes, days = pcs_ref.shape
    n = days // SIDE
    ahead = n // 2 + 1
    for i in range(n):
        for j in range(ahead):
            k = (i + j) % n
            at = (i * ahead + j) * SIDE
            block = rows_ref[at : at + SIDE] * (1.0 / days)
            products_ref[i * SIDE : (i + 1) * SIDE, k * SIDE : (k + 1) * SIDE] = block
            if j:
                products_ref[k * SIDE : (k + 1) * SIDE, i * SIDE : (i + 1) * SIDE] = block.T
    at = n * ahead * SIDE
    for i in range(n):
        pcs_ref[:, i * SIDE : (i + 1) * SIDE] = rows_ref[at : at + modes]
        at += modes
    raw = dot(pcs_ref[...], products_ref[...], NN)
    raw_ref[...] = raw
    high, low = split(raw * (1.0 / days))
    both = jnp.concatenate([high, low], axis=0)
    by_high = one_pass(both, high_ref[...], NN)
    by_low = one_pass(high, low_ref[...], NN)
    cover = by_high[:modes] + by_high[modes:] + by_low
    cover_ref[...] = cover[:, : cover_ref.shape[1]]


def inverse_factor(gram, modes):
    row = lax.broadcasted_iota(jnp.int32, gram.shape, 0)
    lane = lax.broadcasted_iota(jnp.int32, gram.shape, 1)
    whole = jnp.where(lane < modes, jnp.where(row == lane, 1.0, 0.0), gram)
    blocks = [whole[at : at + 8] for at in range(0, modes, 8)]
    sub = lax.broadcasted_iota(jnp.int32, (8, gram.shape[1]), 0)
    for j in range(modes):
        own, at = divmod(j, 8)
        pivot_row = blocks[own][at : at + 1]
        scaled = pivot_row / pivot_row[:, modes + j : modes + j + 1]
        for b in range(own, modes // 8):
            if b == own and at == 7:
                continue
            column = blocks[b][:, modes + j : modes + j + 1]
            step = column * scaled
            if b == own:
                step = jnp.where(sub > at, step, 0.0)
            blocks[b] = blocks[b] - step
    whole = jnp.concatenate(blocks, axis=0)
    pivots = jnp.sum(jnp.where(lane == row + modes, whole, 0.0), axis=1, keepdims=True)
    return jnp.where(lane < modes, whole / jnp.sqrt(pivots), 0.0)


def chain_kernel(products_ref, pcs_ref, raw_ref, both_ref, last_ref):
    modes, days = pcs_ref.shape
    nothing = jnp.zeros((modes, days), F32)
    raw = raw_ref[...]
    gram = dot(pcs_ref[...], jnp.concatenate([nothing, raw]), NT) * (1.0 / days)
    first = inverse_factor(gram, modes)
    pcs = dot(first, jnp.concatenate([raw, nothing]), NN)
    raw = dot(pcs, products_ref[...], NN)
    gram = dot(pcs, jnp.concatenate([nothing, raw]), NT) * (1.0 / days)
    second = inverse_factor(gram, modes)
    last_ref[...] = dot(second, jnp.concatenate([raw, nothing]), NN)
    both_ref[...] = dot(second, jnp.concatenate([first, jnp.zeros_like(first)]), NN)


def call(kernel, shapes, *arrays, flops, spaces=None):
    whole = pl.BlockSpec(memory_space=pltpu.VMEM)
    size = sum(a.size * a.dtype.itemsize for a in arrays)
    size += sum(a.size * a.dtype.itemsize for a in shapes)
    return pl.pallas_call(
        kernel,
        out_shape=shapes,
        in_specs=spaces or [whole] * len(arrays),
        out_specs=[whole] * len(shapes),
        cost_estimate=pl.CostEstimate(flops=flops, bytes_accessed=size, transcendentals=0),
        compiler_params=pltpu.CompilerParams(vmem_limit_bytes=40 * 2**20),
        interpret=INTERPRET,
    )(*arrays)


def local(fields, month_label, row_index, area_table, basis):
    days, lat, lon = fields.shape
    groups = lax.axis_size("days")
    me = lax.axis_index("days")
    wide = -(-(lon + 1) // LANES) * LANES
    modes = basis.shape[0]
    total = days * groups
    n = total // SIDE
    shape = jax.ShapeDtypeStruct

    label = month_label.astype(F32)[None, :, None]
    rows = jnp.pad(jnp.swapaxes(fields, 0, 1).astype(F32), ((0, 0), (0, 0), (0, wide - lon)))
    rows = jnp.where(lax.broadcasted_iota(jnp.int32, rows.shape, 2) == lon, label, rows)
    rows = lax.all_to_all(rows, "days", 0, 0, tiled=True).reshape(total, wide)

    table_row = lax.dynamic_index_in_dim(row_index, me, keepdims=False)
    area = jnp.sum(jnp.where(jnp.arange(area_table.shape[0]) == table_row, area_table, 0.0))
    start = lax.dynamic_index_in_dim(basis, me, axis=1, keepdims=False)
    start = jnp.pad(start, ((0, 0), (0, wide - lon)))

    count = n * (n // 2 + 1) * SIDE + n * modes
    devices = groups * lax.axis_size(SPACE)
    count += -count % devices
    vmem = pl.BlockSpec(memory_space=pltpu.VMEM)
    pieces, high, low = call(
        functools.partial(products_kernel, lon),
        [shape((count, LANES), F32), shape((total, wide), BF16), shape((total, wide), BF16)],
        rows, start, jnp.sqrt(area).reshape(1, 1),
        flops=2 * 3 * total * (total + modes) * wide,
        spaces=[vmem, vmem, pl.BlockSpec(memory_space=pltpu.SMEM)],
    )
    pieces = total_everywhere(pieces)
    products, pcs, raw, cover = call(
        cover_kernel,
        [shape((total, total), F32), shape((modes, total), F32), shape((modes, total), F32),
         shape((modes, lon), F32)],
        pieces, high, low,
        flops=2 * 3 * modes * total * (total + wide),
    )
    cover = to_each(cover, "days")
    both, last = call(
        chain_kernel,
        [shape((modes, 2 * modes), F32), shape((modes, total), F32)],
        products, pcs, raw,
        flops=2 * 6 * modes * total * (total + 8 * modes),
    )
    eofs = jnp.einsum("kj,ljc->klc", both[:, :modes], cover, precision=HIGH)
    return (eofs, lax.dynamic_slice_in_dim(last, me * days, days, axis=1).T)


def solution(mesh):
    space = mesh.shape["space"]
    cores = 2
    around = 4 if space % 8 == 0 else 1
    parts = Mesh(
        mesh.devices.reshape(mesh.shape["days"], space // around // cores, around, cores),
        ("days", *SPACE),
    )
    placed = (
        P("days", SPACE, None), P("days"), P(SPACE), P(), P(None, SPACE, None),
    )
    return jax.shard_map(
        local,
        mesh=parts,
        in_specs=placed,
        out_specs=(P(None, SPACE, None), P("days", None)),
        check_vma=False,
    )
```

time: 224 us -> 174 us (0.78)
  matrix products: 32.5 us -> 2.87 us
  Pallas kernels: 0 us -> 24.1 us
  other arithmetic: 30.4 us -> 6.79 us
  waiting for transfers between devices: 63.5 us -> 47.7 us
  local copies, waits for them, and re-layouts: 16.6 us -> 9.74 us
  blocking collectives: 65 us -> 71.3 us
  starting transfers between devices: 12.7 us -> 9.81 us
    dot_general x27 -> x1, matrix products: 32 us -> 2.87 us  [local(): eofs = jnp.einsum('kj,ljc->klc', both[:, :modes], cover, precision=HIGH)]
    another operation x10 -> x0, other arithmetic: 24.1 us -> none  [the longest x6 13 us: local(): jnp.linalg.cholesky(dot(pcs, raw, ((1,), (1,))) / days_total)]
    pallas_call x0 -> x3, Pallas kernels: none -> 24.1 us  [call(): pl.pallas_call(kernel, out_shape=shapes, in_specs=spaces or [whole] * len...]
    all_to_all x2 -> x1, waiting for transfers between devices: 22.2 us -> 6.41 us  [to_each(): lax.all_to_all(jnp.broadcast_to(shard[None], (devices, *shard.shape)), ax...]
    all_to_all x1 -> x3, blocking collectives: 18.3 us -> 31.8 us  [to_each(): lax.all_to_all(jnp.broadcast_to(shard[None], (devices, *shard.shape)), ax...]
    all_to_all x2 -> x3, blocking collectives: 46.6 us -> 39.5 us  [total_everywhere(): tiles = lax.all_to_all(rows.reshape(shape), axis, 0, 0, tiled=True)]
    all_to_all x2 -> x1, starting transfers between devices: 7.57 us -> 4.68 us  [to_each(): lax.all_to_all(jnp.broadcast_to(shard[None], (devices, *shard.shape)), ax...]
    select_n x0 -> x1, other arithmetic: none -> 2.5 us  [local(): jnp.where(lax.broadcasted_iota(jnp.int32, rows.shape, 2) == lon, label, r...]
  transfers between devices with their start and end apart: 3 -> 2, of which waited for: 3 -> 2; matrix products, arithmetic and copies ran while one was open for 7% -> 2% of each run, Pallas kernels for 0% -> 8%
where the time goes in v1:
time: 174 us
  blocking collectives  71.3 us (41%)
  waiting for transfers between devices  47.7 us (27%)
  Pallas kernels  24.1 us (14%)
  starting transfers between devices  9.81 us (6%)
  local copies, waits for them, and re-layouts  9.74 us (6%)
  other arithmetic  6.79 us (4%)
  matrix products  2.87 us (2%)
    all_to_all x1, waiting for transfers between devices, local(): rows = lax.all_to_all(rows, 'days', 0, 0, tiled=True).reshape(total, wide)  41.3 us
    all_to_all x3, blocking collectives, total_everywhere(): tiles = lax.all_to_all(rows.reshape(shape), axis, 0, 0, tiled=True)  39.5 us
    all_to_all x3, blocking collectives, to_each(): lax.all_to_all(jnp.broadcast_to(shard[None], (devices, *shard.shape)), ax...  31.8 us
    pallas_call x3, Pallas kernels, call(): pl.pallas_call(kernel, out_shape=shapes, in_specs=spaces or [whole] * len...  24.1 us
    unnamed x17, local copies, waits for them, and re-layouts  6.54 us
    all_to_all x1, waiting for transfers between devices, to_each(): lax.all_to_all(jnp.broadcast_to(shard[None], (devices, *shard.shape)), ax...  6.41 us
    all_to_all x1, starting transfers between devices, local(): rows = lax.all_to_all(rows, 'days', 0, 0, tiled=True).reshape(total, wide)  5.13 us
    all_to_all x1, starting transfers between devices, to_each(): lax.all_to_all(jnp.broadcast_to(shard[None], (devices, *shard.shape)), ax...  4.68 us
  transfers between devices with their start and end apart: 2, of which 2 were waited for; matrix products, arithmetic and copies ran while one was open for 2% of the time, Pallas kernels for 8%

profile of v1, /device:TPU:1, one launch (start us, length us, event | category | flops | bytes accessed | tf_op | source)
XLA Modules:
  0.0 173.8 jit_solution(8908092737069300727)
XLA Ops:
  0.6 0.0 copy-start
  0.7 0.8 convert_element_type.11
  1.4 1.9 %copy.22 = bf16[160,4,1440]{2,0,1:T(8,128)(2,1)S(1)} copy(bf16[160,4,1440]{2,1,0:T(4,128)(2,1)} %param.5) | data formatting | bytes 3686400 | tf_op args[0]
  3.3 2.5 %convert_select_fusion = f32[4,160,1536]{2,1,0:T(8,128)} fusion(bf16[4,160,1440]{2,1,0:T(8,128)(2,1)S(1)} %bitcast.23, f32[160]{0:T(256)S(1)} %convert_element_type.11, pred[1536]{0:T(1024)(128)(4,1)S(1)} %iota_compare_fusion), kind=kLoop, calls=%fused_computation | loop fusion | flops 1966080 | bytes 5777536 | tf_op jit(solution)/shard_map/jit(_where)/select_n | solution.py:205
  5.8 0.0 copy-start.6
  5.8 0.0 copy-start.5
  5.8 5.1 %all-to-all-start = ((f32[4,160,1536]{2,1,0:T(8,128)}), f32[4,160,1536]{2,1,0:T(8,128)}, u32[]{:S(2)}, u32[]{:S(2)}) async-start(f32[4,160,1536]{2,1,0:T(8,128)} %convert_select_fusion), calls=%async_computation | async-start | bytes 7864320 | tf_op jit(solution)/shard_map/all_to_all | solution.py:206
  10.9 0.0 copy-done.6
  10.9 0.6 dynamic_slice.12
  11.5 0.0 copy-done.5
  11.5 1.2 fusion.3
  13.5 0.0 copy-done
  13.5 0.4 constant_dynamic-slice_fusion
  13.9 41.3 %all-to-all-done = f32[4,160,1536]{2,1,0:T(8,128)} async-done(((f32[4,160,1536]{2,1,0:T(8,128)}), f32[4,160,1536]{2,1,0:T(8,128)}, u32[]{:S(2)}, u32[]{:S(2)}) %all-to-all-start) | async-done | bytes 3932192 | tf_op jit(solution)/shard_map/all_to_all | solution.py:206
  55.2 9.2 %shard_map.68 = (f32[2304,128]{1,0:T(8,128)S(1)}, bf16[640,1536]{1,0:T(8,128)(2,1)S(1)}, bf16[640,1536]{1,0:T(8,128)(2,1)S(1)}) custom-call(f32[640,1536]{1,0:T(8,128)} %bitcast.1.rows_ref, bf16[64,1536]{1,0:T(8,128)(2,1)S(1)} %pad.13.base_ref, f32[1,1]{1,0:T(1,128)} %bitcast.4.scale_ref), custom_call_target="tpu_custom_call" | custom-call | flops 4152360960 | bytes 9240580 | tf_op jit(solution)/shard_map/pallas_call | solution.py:182
  64.4 0.0 copy-start.1
  64.5 1.3 copy-done.1
  65.7 8.4 %all_to_all.40 = f32[2,1152,128]{2,1,0:T(8,128)} all-to-all(f32[2,1152,128]{2,1,0:T(8,128)S(1)} %bitcast.22), channel_id=1, replica_groups=mesh['days'=4,'z'=8,'x'=4,'core'=2] {'core'}, dimensions={0} | all-to-all | bytes 2359296 | tf_op jit(solution)/shard_map/all_to_all | solution.py:33
  74.2 2.2 %reduce_sum.37 = f32[1152,128]{1,0:T(8,128)} reduce(f32[2,1152,128]{2,1,0:T(8,128)} %all_to_all.40, f32[]{:T(128)} %constant.26.clone.1), dimensions={0}, to_apply=%region_1.2 | reduce | flops 147456 | bytes 1769476 | tf_op jit(solution)/shard_map/reduce_sum | solution.py:34
  76.4 16.2 %all_to_all.41 = f32[16,72,128]{2,1,0:T(8,128)S(1)} all-to-all(f32[16,72,128]{2,1,0:T(8,128)} %bitcast.25), channel_id=1, replica_groups=mesh['days'=4,'z'=8,'x'=4,'core'=2] {'days','x'}, dimensions={0} | all-to-all | bytes 1179648 | tf_op jit(solution)/shard_map/all_to_all | solution.py:33
  92.6 14.9 %all_to_all.42 = f32[8,1,1152]{2,1,0:T(1,128)S(1)} all-to-all(f32[8,1,1152]{2,1,0:T(1,128)S(1)} %bitcast.27), channel_id=1, replica_groups=mesh['days'=4,'z'=8,'x'=4,'core'=2] {'z'}, dimensions={0} | all-to-all | bytes 73728 | tf_op jit(solution)/shard_map/all_to_all | solution.py:33
  107.6 9.3 %all_to_all.43 = f32[8,1,1152]{2,1,0:T(1,128)S(1)} all-to-all(f32[8,1,1152]{2,1,0:T(1,128)S(1)} %broadcast_in_dim.40), channel_id=1, replica_groups=mesh['days'=4,'z'=8,'x'=4,'core'=2] {'z'}, dimensions={0} | all-to-all | bytes 73728 | tf_op jit(solution)/shard_map/all_to_all | solution.py:23
  116.9 12.6 %all_to_all.44 = f32[16,72,128]{2,1,0:T(8,128)S(1)} all-to-all(f32[16,72,128]{2,1,0:T(8,128)S(1)} %broadcast_in_dim.42), channel_id=1, replica_groups=mesh['days'=4,'z'=8,'x'=4,'core'=2] {'days','x'}, dimensions={0} | all-to-all | bytes 1179648 | tf_op jit(solution)/shard_map/all_to_all | solution.py:23
  129.6 0.0 copy-start.2
  129.6 0.1 broadcast_in_dim.44
  129.7 9.8 %all_to_all.45 = f32[2,1152,128]{2,1,0:T(8,128)S(1)} all-to-all(f32[2,1152,128]{2,1,0:T(8,128)S(1)} %broadcast_in_dim.44), channel_id=1, replica_groups=mesh['days'=4,'z'=8,'x'=4,'core'=2] {'core'}, dimensions={0} | all-to-all | bytes 2359296 | tf_op jit(solution)/shard_map/all_to_all | solution.py:23
  139.5 0.0 copy-done.2
  139.5 1.7 shard_map.69
  141.2 0.0 copy-start.3
  141.2 1.2 copy-done.3
  142.4 1.3 broadcast_in_dim.45
  143.7 0.0 copy-start.4
  143.7 4.7 %all-to-all-start.7 = ((f32[4,64,1440]{2,1,0:T(8,128)}), f32[4,64,1440]{2,1,0:T(8,128)}, u32[]{:S(2)}, u32[]{:S(2)}) async-start(f32[4,64,1440]{2,1,0:T(8,128)} %broadcast_in_dim.45), calls=%async_computation.7 | async-start | bytes 3145728 | tf_op jit(solution)/shard_map/all_to_all | solution.py:23
  148.4 0.0 copy-done.4
  148.4 13.2 %shard_map.70 = (f32[64,128]{1,0:T(8,128)S(1)}, f32[64,640]{1,0:T(8,128)S(1)}) custom-call(f32[640,640]{1,0:T(8,128)S(1)} %copy-done.4, f32[64,640]{1,0:T(8,128)S(1)} %get-tuple-element.15.pcs_ref, f32[64,640]{1,0:T(8,128)S(1)} %get-tuple-element.16.raw_ref), custom_call_target="tpu_custom_call" | custom-call | flops 566231040 | bytes 2162688 | tf_op jit(solution)/shard_map/pallas_call | solution.py:182
  161.6 0.7 dynamic-slice_bitcast_fusion
  162.3 6.4 %all-to-all-done.7 = f32[4,64,1440]{2,1,0:T(8,128)} async-done(((f32[4,64,1440]{2,1,0:T(8,128)}), f32[4,64,1440]{2,1,0:T(8,128)}, u32[]{:S(2)}, u32[]{:S(2)}) %all-to-all-start.7) | async-done | bytes 1474592 | tf_op jit(solution)/shard_map/all_to_all | solution.py:23
  168.7 2.9 %fusion = f32[64,4,1440]{2,0,1:T(8,128)S(1)} fusion(f32[4,64,1440]{2,1,0:T(8,128)} %all-to-all-done.7, f32[64,128]{1,0:T(8,128)S(1)} %get-tuple-element.17), kind=kOutput, calls=%fused_computation.4 | convolution fusion | flops 283115520 | bytes 2981888 | tf_op jit(solution)/shard_map/kj,ljc->klc/dot_general | solution.py:239
  171.6 2.2 %copy.18 = f32[64,4,1440]{2,1,0:T(4,128)} copy(f32[64,4,1440]{2,0,1:T(8,128)S(1)} %fusion) | data formatting | bytes 2949120
  (7 shorter events, 0.2 us)
Async XLA Ops:
  0.6 12.8 %copy-start = (bf16[64,4,1440]{2,1,0:T(4,128)(2,1)S(1)}, bf16[64,4,1440]{2,1,0:T(4,128)(2,1)}, u32[]{:S(2)}) copy-start(bf16[64,4,1440]{2,1,0:T(4,128)(2,1)} %param.9) | copy-start | bytes 2211844
  5.8 5.1 %copy-start.6 = (s32[4]{0:T(128)S(1)}, s32[4]{0:T(128)}, u32[]{:S(2)}) copy-start(s32[4]{0:T(128)} %param.7) | copy-start | bytes 52
  5.8 5.7 %copy-start.5 = (f32[256]{0:T(256)S(1)}, f32[256]{0:T(256)}, u32[]{:S(2)}) copy-start(f32[256]{0:T(256)} %param.8) | copy-start | bytes 3076
  5.8 49.4 %all-to-all-start = ((f32[4,160,1536]{2,1,0:T(8,128)}), f32[4,160,1536]{2,1,0:T(8,128)}, u32[]{:S(2)}, u32[]{:S(2)}) async-start(f32[4,160,1536]{2,1,0:T(8,128)} %convert_select_fusion), calls=%async_computation | async-start | bytes 7864320 | tf_op jit(solution)/shard_map/all_to_all | solution.py:206
  64.4 1.3 copy-start.1
  129.6 9.9 %copy-start.2 = (bf16[640,1536]{1,0:T(8,128)(2,1)S(1)}, bf16[640,1536]{1,0:T(8,128)(2,1)}, u32[]{:S(2)}) copy-start(bf16[640,1536]{1,0:T(8,128)(2,1)} %copy-done.1) | copy-start | bytes 5898244
  141.2 1.2 copy-start.3
  143.7 4.7 %copy-start.4 = (f32[640,640]{1,0:T(8,128)S(1)}, f32[640,640]{1,0:T(8,128)}, u32[]{:S(2)}) copy-start(f32[640,640]{1,0:T(8,128)} %copy-done.3) | copy-start | bytes 4915204
  143.7 25.0 %all-to-all-start.7 = ((f32[4,64,1440]{2,1,0:T(8,128)}), f32[4,64,1440]{2,1,0:T(8,128)}, u32[]{:S(2)}, u32[]{:S(2)}) async-start(f32[4,64,1440]{2,1,0:T(8,128)} %broadcast_in_dim.45), calls=%async_computation.7 | async-start | bytes 3145728 | tf_op jit(solution)/shard_map/all_to_all | solution.py:23
